TPU v7x, 32 devices: a whole 2x2x4 slice. The times are simulated.
32 devices in a mesh: groups: 2 (over y), tiles: 16 (over z, x, core).
Axes of the slice: x: 2, y: 2, z: 4, core: 2. Of those that a mesh axis runs over, the one named last changes fastest.
Arguments:
- raw: bfloat16 [16, 256, 2048], P(None, ('groups', 'tiles')), parts along dimension 1, may hold values from -40 to 40, as said below
- fir: float32 [64], replicated, may hold values from -0.75 to 0.75
- keep: int32 [16, 256], P(None, ('groups', 'tiles')), parts along dimension 1, may hold values 0 or 1
- table: int32 [16, 2], replicated, may hold values from 0 to 0, as said below
Outputs:
- stacks: bfloat16 [32, 128, 128, 256], P(('groups', 'tiles')), parts along dimension 0
There are 2 independent parts, one for each index of `groups`. A program takes and returns all parts, laid end to end along the dimension named above; an argument that names none is the same for every part. Nothing has to cross between parts.
Inputs may be any that keep to these rules, and one draw needn't show every extreme that they name: `table`: each row holds r <= c. `raw`: a common motion of all channels plus independent noise.
All inputs are finite; a program needn't handle non-finite values. No bound on the sum of `keep` on one device may be relied on, other than what follows from the above.
Results may differ from a plain program's by a relative error of at most 0.0053.
Values may be sent and summed in bfloat16 or wider, within the bound.
A program may use at most 128 MiB of HBM per device.

v0:
```python
import jax
import jax.numpy as jnp
from jax import lax
from jax.sharding import PartitionSpec as P

WINDOWS = 16
TILE = 128
SEG = 512
LAGS = 256
TAPS = 64
DEC = 4
RAW = 2048
NBIN = 256


def filter_band(fir):
    period = 2 * RAW + TAPS
    pattern = jnp.concatenate([fir[:1], jnp.zeros((period - TAPS,), jnp.float32), fir[1:][::-1]])
    tiled = jnp.tile(pattern, SEG)[: SEG * (period - DEC)].reshape(SEG, period - DEC)
    return tiled[:, :RAW]


def filter_block(raw, fir):
    band = filter_band(fir)
    return jnp.einsum("wcm,nm->wcn", raw.astype(jnp.float32), band, precision=lax.Precision.HIGHEST)


def dft_tables():
    steps = jnp.arange(SEG, dtype=jnp.int32)
    freqs = jnp.arange(NBIN, dtype=jnp.int32)
    angle = 2.0 * jnp.pi / SEG * jnp.mod(steps[:, None] * freqs[None, :], SEG).astype(jnp.float32)
    return (jnp.cos(angle), jnp.sin(angle))


def whiten(decimated, keep):
    cosine, sine = dft_tables()
    real_part = jnp.einsum("wcn,nf->wcf", decimated, cosine, precision=lax.Precision.HIGHEST)
    imag_part = -jnp.einsum("wcn,nf->wcf", decimated, sine, precision=lax.Precision.HIGHEST)
    power = real_part * real_part + imag_part * imag_part
    level = jnp.mean(power, -1, keepdims=True)
    scale = keep.astype(jnp.float32)[..., None] / jnp.sqrt(0.5 * power + 0.5 * level + 1e-05)
    return jnp.concatenate([real_part * scale, imag_part * scale], -1).astype(jnp.bfloat16)


def cross_tile(rows, cols):
    half = rows.shape[-1] // 2
    row_re, row_im = (rows[..., :half], rows[..., half:])
    col_re, col_im = (cols[..., :half], cols[..., half:])
    cross_re = jnp.einsum("wif,wjf->ijf", row_re, col_re, preferred_element_type=jnp.float32)
    cross_re = cross_re + jnp.einsum(
        "wif,wjf->ijf", row_im, col_im, preferred_element_type=jnp.float32
    )
    cross_im = jnp.einsum("wif,wjf->ijf", row_re, col_im, preferred_element_type=jnp.float32)
    cross_im = cross_im - jnp.einsum(
        "wif,wjf->ijf", row_im, col_re, preferred_element_type=jnp.float32
    )
    return jnp.concatenate([cross_re, cross_im], -1).astype(jnp.bfloat16)


def lag_rows(freqs, imaginary):
    shifts = jnp.arange(LAGS, dtype=jnp.int32) - LAGS // 2
    angle = 2.0 * jnp.pi / SEG * jnp.mod(freqs[:, None] * shifts[None, :], SEG).astype(jnp.float32)
    weight = jnp.where(freqs == 0, 1.0, 2.0).astype(jnp.float32)[:, None] / jnp.sqrt(
        jnp.float32(WINDOWS * NBIN)
    )
    return jnp.where(imaginary[:, None], -weight * jnp.sin(angle), weight * jnp.cos(angle)).astype(
        jnp.bfloat16
    )


def local(raw, fir, keep, table):
    devices = lax.axis_size("tiles")
    filtered = filter_block(raw, fir)
    channel_sum = lax.psum(jnp.sum(filtered, 1), "tiles")
    common = channel_sum[:, None, :] / (raw.shape[1] * devices)
    whitened = whiten(filtered - common, keep)
    entry = table[lax.axis_index("tiles")]
    row_base = entry[0] * TILE
    col_base = entry[1] * TILE
    offsets = jnp.arange(TILE, dtype=jnp.int32)
    piece = lax.all_gather(whitened, "tiles", axis=1, tiled=True)
    places = jnp.arange(piece.shape[1], dtype=jnp.int32)
    pick_rows = (places[None, :] == row_base + offsets[:, None]).astype(jnp.bfloat16)
    pick_cols = (places[None, :] == col_base + offsets[:, None]).astype(jnp.bfloat16)
    add_rows = jnp.einsum("in,wnf->wif", pick_rows, piece, preferred_element_type=jnp.float32)
    add_cols = jnp.einsum("in,wnf->wif", pick_cols, piece, preferred_element_type=jnp.float32)
    rows = add_rows.astype(jnp.bfloat16)
    cols = add_cols.astype(jnp.bfloat16)
    cross = cross_tile(rows, cols).reshape(TILE * TILE, 2 * NBIN)
    freqs = jnp.concatenate([jnp.arange(NBIN, dtype=jnp.int32)] * 2)
    imaginary = jnp.arange(2 * NBIN, dtype=jnp.int32) >= NBIN
    lags = lag_rows(freqs, imaginary)
    stacked = jnp.dot(cross, lags, preferred_element_type=jnp.float32).astype(jnp.bfloat16)
    return stacked.reshape(1, TILE, TILE, LAGS)


def solution(mesh):
    placed = (P(None, ("groups", "tiles"), None), P(), P(None, ("groups", "tiles")), P())
    return jax.shard_map(
        local,
        mesh=mesh,
        in_specs=placed,
        out_specs=P(("groups", "tiles"), None, None, None),
        check_vma=False,
    )
```

profile of v0, /device:TPU:0, one launch (start us, length us, event | category | flops | bytes accessed | tf_op | source)
XLA Modules:
  0.0 251.8 jit_solution(16928799047254272326)
XLA Ops:
  6.5 0.0 all-gather.2.cloned.1.call-start
  6.5 0.8 slice.33
  7.3 0.1 rev.3
  7.4 0.7 concatenate.26
  8.2 3.9 %tile.4 = f32[512,4160]{1,0:T(8,128)} broadcast(f32[4160]{0:T(1024)S(1)} %concatenate.26), dimensions={1} | broadcast | bytes 8536320 | tf_op jit(solution)/shard_map/tile | solution.py:19
  12.0 10.0 %tile.10 = f32[2129920]{0:T(1024)} reshape(f32[512,4160]{1,0:T(8,128)} %tile.4) | data formatting | bytes 17039360 | tf_op jit(solution)/shard_map/tile | solution.py:19
  22.0 7.8 %slice.42 = f32[2127872]{0:T(1024)} slice(f32[2129920]{0:T(1024)} %tile.10), slice={[0:2127872]} | slice | bytes 17022976 | tf_op jit(solution)/shard_map/slice | solution.py:19
  29.8 14.4 %reshape.66 = f32[512,4156]{1,0:T(8,128)} reshape(f32[2127872]{0:T(1024)} %slice.42) | data formatting | bytes 17022976 | tf_op jit(solution)/shard_map/reshape | solution.py:19
  44.1 0.0 copy-done
  44.2 4.8 %fusion.70 = (f32[16,512]{1,0:T(8,128)S(1)}, f32[16,8,512]{2,0,1:T(8,128)S(1)}) fusion(bf16[16,8,2048]{2,1,0:T(8,128)(2,1)S(1)} %copy-done, f32[512,4156]{1,0:T(8,128)} %reshape.66), kind=kOutput, calls=%fused_computation.98 | convolution fusion | flops 1610670080 | bytes 5013504 | tf_op jit(solution)/shard_map/wcm,nm->wcn/dot_general | solution.py:25
  49.0 62.9 %psum.7 = f32[16,512]{1,0:T(8,128)S(1)} all-reduce(f32[16,512]{1,0:T(8,128)S(1)} %get-tuple-element.15), channel_id=1, replica_groups=mesh['groups'=2,'tiles'=16] {'tiles'}, use_global_device_ids=true, to_apply=%region_1.0 | all-reduce | flops 8192 | bytes 65536 | tf_op jit(solution)/shard_map/psum | solution.py:74
  112.0 2.4 fusion.25
  114.4 2.5 fusion.46
  116.9 0.0 copy-done.2
  116.9 0.1 copy.19
  117.0 0.1 multiply_convert_fusion.1
  117.1 0.7 pad_maximum_fusion
  117.7 0.0 all-gather.2.cloned.1.call-update
  117.8 0.0 copy-done.3
  117.8 0.1 constant_dynamic-slice_fusion
  117.9 0.6 fusion.69
  119.8 36.6 %all-gather.2.cloned.1.call-done = bf16[16,128,512]{2,1,0:T(8,128)(2,1)} async-done(((bf16[16,8,512]{2,1,0:T(8,128)(2,1)}), bf16[16,128,512]{2,1,0:T(8,128)(2,1)}) %all-gather.2.cloned.1.call-update) | async-done | bytes 2097168 | tf_op jit(solution)/shard_map/all_gather | solution.py:81
  156.4 2.4 convert_bitcast_fusion
  158.8 2.4 convert_bitcast_fusion.1
  161.2 0.3 fusion.67
  161.5 8.1 %fusion.13 = f32[256,128,128]{2,1,0:T(8,128)} fusion(bf16[16,128,256]{1,2,0:T(8,128)(2,1)S(1)} %get-tuple-element.19, bf16[16,128,256]{1,2,0:T(8,128)(2,1)S(1)} %get-tuple-element.5), kind=kOutput, calls=%fused_computation.22 | convolution fusion | flops 134217728 | bytes 18874368 | tf_op jit(solution)/shard_map/wif,wjf->ijf/dot_general | solution.py:49
  169.6 8.1 %fusion.9 = f32[256,128,128]{2,1,0:T(8,128)} fusion(bf16[16,128,256]{1,2,0:T(8,128)(2,1)S(1)} %get-tuple-element.6, bf16[16,128,256]{1,2,0:T(8,128)(2,1)S(1)} %get-tuple-element.19), kind=kOutput, calls=%fused_computation.18 | convolution fusion | flops 134217728 | bytes 18874368 | tf_op jit(solution)/shard_map/wif,wjf->ijf/dot_general | solution.py:53
  177.6 12.9 %fusion.3 = bf16[128,128,256]{0,1,2:T(8,128)(2,1)} fusion(f32[256,128,128]{2,1,0:T(8,128)} %fusion.13, bf16[16,128,256]{1,2,0:T(8,128)(2,1)S(1)} %get-tuple-element.20, bf16[16,128,256]{1,2,0:T(8,128)(2,1)S(1)} %get-tuple-element.6), kind=kOutput, calls=%fused_computation.6 | convolution fusion | flops 142606336 | bytes 27262976 | tf_op jit(solution)/shard_map/wif,wjf->ijf/dot_general | solution.py:50
  190.5 13.5 %copy.25 = bf16[128,128,256]{2,1,0:T(8,128)(2,1)} copy(bf16[128,128,256]{0,1,2:T(8,128)(2,1)} %fusion.3) | data formatting | bytes 16777216 | tf_op jit(solution)/shard_map/add | solution.py:50
  204.0 12.9 %fusion.4 = bf16[128,128,256]{0,1,2:T(8,128)(2,1)} fusion(f32[256,128,128]{2,1,0:T(8,128)} %fusion.9, bf16[16,128,256]{1,2,0:T(8,128)(2,1)S(1)} %get-tuple-element.20, bf16[16,128,256]{1,2,0:T(8,128)(2,1)S(1)} %get-tuple-element.5), kind=kOutput, calls=%fused_computation.7 | convolution fusion | flops 142606336 | bytes 27262976 | tf_op jit(solution)/shard_map/wif,wjf->ijf/dot_general | solution.py:54
  216.9 13.5 %copy.30 = bf16[128,128,256]{2,1,0:T(8,128)(2,1)} copy(bf16[128,128,256]{0,1,2:T(8,128)(2,1)} %fusion.4) | data formatting | bytes 16777216 | tf_op jit(solution)/shard_map/sub | solution.py:54
  230.4 14.5 %convolution_convert_fusion = bf16[16384,256]{1,0:T(8,128)(2,1)} fusion(bf16[16384,256]{1,0:T(8,128)(2,1)} %bitcast.40, bf16[16384,256]{1,0:T(8,128)(2,1)} %bitcast.39, f32[512]{0:T(512)S(1)} %get-tuple-element.12, s32[256]{0:T(256)S(1)} %iota_add_fusion, s32[512]{0:T(512)S(1)} %pad_add_fusion, f32[512]{0:T(512)S(1)} %get-tuple-element.11, ...), kind=kOutput, calls=%fused_computation | convolution fusion | flops 4335075328 | bytes 25173504 | tf_op jit(solution)/shard_map/dot_general | solution.py:93
  (17 shorter events, 0.1 us)
Async XLA Ops:
  6.5 37.6 %copy-start = (bf16[16,8,2048]{2,1,0:T(8,128)(2,1)S(1)}, bf16[16,8,2048]{2,1,0:T(8,128)(2,1)}, u32[]{:S(2)}) copy-start(bf16[16,8,2048]{2,1,0:T(8,128)(2,1)} %param.4) | copy-start | bytes 1572868
  6.5 149.9 %all-gather.2.cloned.1.call-start = ((), (), s32[]{:S(2)}) async-start(), calls=%async_computation | async-start | bytes 2228224 | tf_op jit(solution)/shard_map/all_gather | solution.py:81
  44.2 72.7 %copy-start.2 = (s32[16,8]{0,1:T(8,128)S(1)}, s32[16,8]{0,1:T(8,128)}, u32[]{:S(2)}) copy-start(s32[16,8]{0,1:T(8,128)} %param.6) | copy-start | bytes 1540
  44.2 73.6 %copy-start.3 = (s32[16,2]{0,1:T(2,128)S(1)}, s32[16,2]{0,1:T(2,128)}, u32[]{:S(2)}) copy-start(s32[16,2]{0,1:T(2,128)} %param.7) | copy-start | bytes 388
  230.4 14.5 %copy-start.1 = (bf16[16,8,2048]{2,1,0:T(8,128)(2,1)S(1)}, bf16[16,8,2048]{2,1,0:T(8,128)(2,1)}, u32[]{:S(2)}) copy-start(bf16[16,8,2048]{2,1,0:T(8,128)(2,1)} %param.4) | copy-start | bytes 1572868
Sparse Core Ops, SparseCore 0:
  117.9 38.4 all-gather.1
where the time goes:
time: 253 us; the launch traced here: 252 us
  matrix products  71 us (28%)
  local copies, waits for them, and re-layouts  65.6 us (26%)
  blocking collectives  62.9 us (25%)
  waiting for transfers between devices  36.6 us (14%)
  between operations  14.8 us (6%)
    psum x1, blocking collectives, local(): channel_sum = lax.psum(jnp.sum(filtered, 1), 'tiles')  62.9 us
    all_gather x1, waiting for transfers between devices, local(): piece = lax.all_gather(whitened, 'tiles', axis=1, tiled=True)  36.6 us
    dot_general x1, matrix products, local(): jnp.dot(cross, lags, preferred_element_type=jnp.float32)  14.5 us
    reshape x1, local copies, waits for them, and re-layouts, filter_band(): jnp.tile(pattern, SEG)[:SEG * (period - DEC)].reshape(SEG, period - DEC)  14.4 us
    another operation x2, local copies, waits for them, and re-layouts, filter_band(): jnp.tile(pattern, SEG)[:SEG * (period - DEC)].reshape(SEG, period - DEC)  13.8 us
    sub x1, local copies, waits for them, and re-layouts, cross_tile(): cross_im - jnp.einsum('wif,wjf->ijf', row_im, col_re, preferred_element_t...  13.5 us
    add x1, local copies, waits for them, and re-layouts, cross_tile(): cross_re + jnp.einsum('wif,wjf->ijf', row_im, col_im, preferred_element_t...  13.5 us
    dot_general x1, matrix products, cross_tile(): jnp.einsum('wif,wjf->ijf', row_im, col_re, preferred_element_type=jnp.flo...  12.9 us
  transfers between devices with their start and end apart: 1, of which 1 were waited for; matrix products, arithmetic and copies ran while one was open for 0% of the time, Pallas kernels for 0%

commit v1 on v0

v1 whole, which is shorter than its diff:
```python
import functools

import jax
import jax.numpy as jnp
import numpy as np
from jax import lax
from jax.experimental import pallas as pl
from jax.experimental.pallas import tpu as pltpu
from jax.sharding import PartitionSpec as P

WINDOWS = 16
TILE = 128
SEG = 512
LAGS = 256
TAPS = 64
DEC = 4
RAW = 2048
NBIN = 256
SPAN = 640
STRIDE = 520


def split2(x):
    high = x.astype(jnp.bfloat16)
    return high, (x - high.astype(jnp.float32)).astype(jnp.bfloat16)


def split3(x):
    high = x.astype(jnp.bfloat16)
    rest = x - high.astype(jnp.float32)
    middle = rest.astype(jnp.bfloat16)
    return high, middle, (rest - middle.astype(jnp.float32)).astype(jnp.bfloat16)


def contract(a, b, left, right):
    return lax.dot_general(a, b, (((left,), (right,)), ((), ())), preferred_element_type=jnp.float32)


def dft_tables():
    angle = 2.0 * np.pi / SEG * np.mod(np.arange(SEG)[:, None] * np.arange(NBIN)[None, :], SEG)
    table = np.concatenate([np.cos(angle), -np.sin(angle)], 1).astype(np.float32)
    high = table.astype(jnp.bfloat16)
    low = (table - high.astype(np.float32)).astype(jnp.bfloat16)
    return jnp.asarray(np.concatenate([high, low], 0))


def lag_table():
    freqs = np.arange(NBIN)
    shifts = np.arange(LAGS) - LAGS // 2
    angle = 2.0 * np.pi / SEG * np.mod(freqs[:, None] * shifts[None, :], SEG)
    weight = np.where(freqs == 0, 1.0, 2.0)[:, None] / np.sqrt(WINDOWS * NBIN)
    table = np.concatenate([weight * np.cos(angle), -weight * np.sin(angle)], 0)
    return jnp.asarray(table.astype(np.float32).astype(jnp.bfloat16))


def filter_rows(raw_ref, taps_ref):
    rows = raw_ref.shape[0] * raw_ref.shape[1]
    raw = raw_ref[...].astype(jnp.float32).reshape(rows, RAW).astype(jnp.bfloat16)
    band = jnp.broadcast_to(taps_ref[...], (TILE, SPAN))
    index = lax.broadcasted_iota(jnp.int32, (TILE, SPAN), 0)
    for bit in range(7):
        band = jnp.where((index >> bit) & 1 == 1, pltpu.roll(band, DEC << bit, 1), band)
    pieces = [jnp.concatenate([jnp.zeros((rows, TILE), jnp.bfloat16), raw[:, :SEG]], 1)]
    for block in range(1, RAW // SEG):
        pieces.append(raw[:, block * SEG - TILE : (block + 1) * SEG])
    spans = jnp.concatenate(pieces, 0)
    out = sum(contract(spans, part, 1, 1) for part in split3(band)[::-1])
    return jnp.concatenate([out[b * rows : (b + 1) * rows] for b in range(RAW // SEG)], 1)


def whiten_rows(decimated, keep, table_ref):
    high, low = split2(decimated)
    table_high = table_ref[:SEG, :]
    spectrum = contract(low, table_high, 1, 0) + contract(high, table_ref[SEG:, :], 1, 0)
    spectrum = spectrum + contract(high, table_high, 1, 0)
    real_part, imag_part = spectrum[:, :NBIN], spectrum[:, NBIN:]
    power = real_part * real_part + imag_part * imag_part
    level = jnp.mean(power, -1, keepdims=True)
    scale = keep.astype(jnp.float32) * lax.rsqrt(0.5 * power + 0.5 * level + 1e-05)
    return jnp.concatenate([real_part * scale, imag_part * scale], 1).astype(jnp.bfloat16)


def arrange(piece_ref, spectra_ref):
    members, rows = piece_ref.shape[:2]
    width = rows // WINDOWS
    for pair in range(WINDOWS // 2):
        for quarter in range(4):
            block = piece_ref[:, pair * 2 * width : (pair + 1) * 2 * width, quarter * 128 : (quarter + 1) * 128]
            block = block.astype(jnp.float32)
            for half in range(2):
                turned = block[:, half * width : (half + 1) * width].reshape(members * width, 128).T
                start = (quarter % 2) * 128 * 32 + (quarter // 2) * WINDOWS + pair * 2 + half
                spectra_ref[pl.ds(start, 128, 32), :] = turned


def stack_kernel(same, per_step, entry_ref, rows_ref, cols_ref, lag_ref, out_ref, row_spec, col_spec, cross_ref):
    @pl.when(pl.program_id(0) == 0)
    def _():
        arrange(rows_ref, row_spec)
        if not same:
            arrange(cols_ref, col_spec)

        def one_bin(f, carry):
            start = pl.multiple_of(f * 32, 32)
            left = row_spec[pl.ds(start, 32), :]
            right = left if same else col_spec[pl.ds(start, 32), :]
            turned = jnp.concatenate([right[WINDOWS:], -right[:WINDOWS]], 0)
            both = jnp.concatenate([right, turned], 1).astype(jnp.bfloat16)
            cross = contract(left.astype(jnp.bfloat16), both, 0, 0)
            cross_ref[pl.ds(f, TILE, STRIDE), :] = cross[:, :TILE]
            cross_ref[pl.ds(f + NBIN, TILE, STRIDE), :] = cross[:, TILE:]
            return carry

        lax.fori_loop(0, NBIN, one_bin, 0, unroll=8)

    base = pl.program_id(0) * per_step
    for group in range(per_step // 4):
        picked = []
        for member in range(4):
            start = pl.multiple_of((base + group * 4 + member) * STRIDE, 8)
            picked.append(cross_ref[pl.ds(start, 2 * NBIN), :].astype(jnp.bfloat16))
        stacked = contract(jnp.concatenate(picked, 1), lag_ref[...], 0, 0)
        out_ref[group * 4 : group * 4 + 4] = stacked.reshape(4, TILE, LAGS).astype(jnp.bfloat16)


def stack(gathered, entry):
    members = TILE * WINDOWS // gathered.shape[1]
    same = gathered.shape[0] == members
    per_step = 8
    block = (members,) + gathered.shape[1:]
    spec_shape = pltpu.VMEM((2 * NBIN * WINDOWS, TILE), jnp.float32)
    small = pltpu.VMEM((8, 128), jnp.float32)
    return pl.pallas_call(
        functools.partial(stack_kernel, same, per_step),
        out_shape=jax.ShapeDtypeStruct((TILE, TILE, LAGS), jnp.bfloat16),
        grid_spec=pltpu.PrefetchScalarGridSpec(
            num_scalar_prefetch=1,
            grid=(TILE // per_step,),
            in_specs=[
                pl.BlockSpec(block, lambda s, entry: (entry[0], 0, 0)),
                pl.BlockSpec((8, 128) if same else block, (lambda s, entry: (0, 0)) if same else (lambda s, entry: (entry[1], 0, 0))),
                pl.BlockSpec((2 * NBIN, LAGS), lambda s, entry: (0, 0)),
            ],
            out_specs=pl.BlockSpec((per_step, TILE, LAGS), lambda s, entry: (s, 0, 0)),
            scratch_shapes=[spec_shape, small if same else spec_shape, pltpu.VMEM((TILE * STRIDE, TILE), jnp.float32)],
        ),
        compiler_params=pltpu.CompilerParams(vmem_limit_bytes=60 << 20),
        cost_estimate=pl.CostEstimate(flops=10 << 30, bytes_accessed=12 << 20, transcendentals=0),
    )(entry, gathered, entry_dummy() if same else gathered, lag_table())


def entry_dummy():
    return jnp.zeros((8, 128), jnp.float32)


def taps_row(fir):
    return jnp.pad(fir[::-1], (TILE + 1 - TAPS, SPAN - TILE - 1))[None, :]


def filter_kernel(raw_ref, taps_ref, filtered_ref, sum_ref):
    filtered = filter_rows(raw_ref, taps_ref)
    filtered_ref[...] = filtered
    sum_ref[...] = jnp.sum(filtered.reshape(raw_ref.shape[0], raw_ref.shape[1], SEG), 1)


def whiten_kernel(channels, filtered_ref, sum_ref, keep_ref, table_ref, out_ref):
    rows = filtered_ref.shape[0]
    width = rows // WINDOWS
    common = sum_ref[...] / channels
    decimated = filtered_ref[...].reshape(WINDOWS, width, SEG) - common[:, None, :]
    out_ref[...] = whiten_rows(decimated.reshape(rows, SEG), keep_ref[...], table_ref)


def local(raw, fir, keep, table):
    devices = lax.axis_size("tiles")
    rows = raw.shape[0] * raw.shape[1]
    filtered, sums = pl.pallas_call(
        filter_kernel,
        out_shape=(jax.ShapeDtypeStruct((rows, SEG), jnp.float32), jax.ShapeDtypeStruct((WINDOWS, SEG), jnp.float32)),
        compiler_params=pltpu.CompilerParams(vmem_limit_bytes=32 << 20),
    )(raw, taps_row(fir))
    sums = lax.psum(sums, "tiles")
    whitened = pl.pallas_call(
        functools.partial(whiten_kernel, raw.shape[1] * devices),
        out_shape=jax.ShapeDtypeStruct((rows, 2 * NBIN), jnp.bfloat16),
        compiler_params=pltpu.CompilerParams(vmem_limit_bytes=32 << 20),
    )(filtered, sums, keep.reshape(rows, 1), dft_tables())
    gathered = lax.all_gather(whitened, "tiles", axis=0)
    entry = table[lax.axis_index("tiles")]
    return stack(gathered, entry)[None]


def solution(mesh):
    placed = (P(None, ("groups", "tiles"), None), P(), P(None, ("groups", "tiles")), P())
    return jax.shard_map(
        local,
        mesh=mesh,
        in_specs=placed,
        out_specs=P(("groups", "tiles"), None, None, None),
        check_vma=False,
    )
```

time: 253 us -> 150 us (0.59)
  matrix products: 71 us -> 0 us
  local copies, waits for them, and re-layouts: 65.6 us -> 5.19 us
  Pallas kernels: 0 us -> 29.8 us
    dot_general x10 -> x0, matrix products: 71 us -> none  [the longest x1 14.5 us: local(): jnp.dot(cross, lags, preferred_element_type=jnp.float32)]
    pallas_call x0 -> x3, Pallas kernels: none -> 29.8 us  [the longest x1 27.5 us: stack(): pl.pallas_call(functools.partial(stack_kernel, same, per_step), out_shape...]
    reshape x1, local copies, waits for them, and re-layouts: 14.4 us -> 0.08 us  [local(): keep.reshape(rows, 1)]
    another operation x2 -> x0, local copies, waits for them, and re-layouts: 13.8 us -> none  [filter_band(): jnp.tile(pattern, SEG)[:SEG * (period - DEC)].reshape(SEG, period - DEC)]
    sub x1 -> x0, local copies, waits for them, and re-layouts: 13.5 us -> none  [cross_tile(): cross_im - jnp.einsum('wif,wjf->ijf', row_im, col_re, preferred_element_t...]
    add x1 -> x0, local copies, waits for them, and re-layouts: 13.5 us -> none  [cross_tile(): cross_re + jnp.einsum('wif,wjf->ijf', row_im, col_im, preferred_element_t...]
    slice x4 -> x0, local copies, waits for them, and re-layouts: 9.45 us -> none  [the longest x1 7.81 us: filter_band(): jnp.tile(pattern, SEG)[:SEG * (period - DEC)].reshape(SEG, period - DEC)]
    unnamed x8 -> x7, local copies, waits for them, and re-layouts: 0.02 us -> 3.02 us
where the time goes in v1:
time: 150 us
  blocking collectives  62.9 us (42%)
  waiting for transfers between devices  38.2 us (25%)
  Pallas kernels  29.8 us (20%)
  between operations  13.4 us (9%)
  local copies, waits for them, and re-layouts  5.19 us (3%)
    psum x1, blocking collectives, local(): sums = lax.psum(sums, 'tiles')  62.9 us
    all_gather x1, waiting for transfers between devices, local(): gathered = lax.all_gather(whitened, 'tiles', axis=0)  38.2 us
    pallas_call x1, Pallas kernels, stack(): pl.pallas_call(functools.partial(stack_kernel, same, per_step), out_shape...  27.5 us
    unnamed x7, local copies, waits for them, and re-layouts  3.02 us
  transfers between devices with their start and end apart: 1, of which 1 were waited for; matrix products, arithmetic and copies ran while one was open for 0% of the time, Pallas kernels for 0%

profile of v1, /device:TPU:0, one launch (start us, length us, event | category | flops | bytes accessed | tf_op | source)
XLA Modules:
  0.0 149.5 jit_solution(2047514831447050193)
XLA Ops:
  6.5 0.0 copy-start
  6.5 0.0 all-gather.3.cloned.1.call-start
  6.5 0.7 rev.3
  7.3 0.1 pad.4
  7.4 0.8 copy.9
  8.1 0.1 reshape.5.keep_ref
  8.2 0.0 copy-start.2
  8.2 1.0 copy-done.2
  9.3 1.1 shard_map.64
  10.4 62.9 %psum.7.sum_ref = f32[16,512]{1,0:T(8,128)S(1)} all-reduce(f32[16,512]{1,0:T(8,128)S(1)} %get-tuple-element.8), channel_id=1, replica_groups=mesh['groups'=2,'tiles'=16] {'tiles'}, use_global_device_ids=true, to_apply=%region_0.1 | all-reduce | flops 8192 | bytes 65536 | tf_op jit(solution)/shard_map/psum | solution.py:182
  73.3 0.0 copy-start.1
  73.3 1.2 copy-done.1
  74.6 1.1 shard_map.65
  75.7 0.0 all-gather.3.cloned.1.call-update
  75.7 0.0 copy-done
  75.7 0.7 dynamic-slice_reduce_fusion.entry_ref
  76.4 38.2 %all-gather.3.cloned.1.call-done = bf16[2048,512]{1,0:T(8,128)(2,1)} async-done(((bf16[128,512]{1,0:T(8,128)(2,1)}), bf16[2048,512]{1,0:T(8,128)(2,1)}) %all-gather.3.cloned.1.call-update) | async-done | bytes 2097168 | tf_op jit(solution)/shard_map/all_gather | solution.py:188
  114.6 0.6 broadcast_in_dim.10.cols_ref
  115.2 27.5 %shard_map.66 = bf16[128,128,256]{2,1,0:T(8,128)(2,1)} custom-call(s32[2]{0:T(128)} %dynamic-slice_reduce_fusion.entry_ref, bf16[16,128,512]{2,1,0:T(8,128)(2,1)} %bitcast.2, f32[8,128]{1,0:T(8,128)} %broadcast_in_dim.10.cols_ref, bf16[512,256]{1,0:T(8,128)(2,1)} %constant.16.clone.lag_ref), custom_call_target="tpu_custom_call" | custom-call | flops 10737418240 | bytes 12582912 | tf_op jit(solution)/shard_map/pallas_call | solution.py:133
  (1 shorter events, 0.0 us)
Async XLA Ops:
  6.5 69.2 %copy-start = (s32[16,2]{0,1:T(2,128)S(1)}, s32[16,2]{0,1:T(2,128)}, u32[]{:S(2)}) copy-start(s32[16,2]{0,1:T(2,128)} %param.9) | copy-start | bytes 388
  6.5 108.0 %all-gather.3.cloned.1.call-start = ((), (), s32[]{:S(2)}) async-start(), calls=%async_computation | async-start | bytes 2228224 | tf_op jit(solution)/shard_map/all_gather | solution.py:188
  8.2 1.0 copy-start.2
  73.3 1.2 copy-start.1
Sparse Core Ops, SparseCore 0:
  75.8 38.6 all-gather.2

commit v2 on v1

--- a/solution.py
+++ b/solution.py
@@ -56,7 +56,11 @@
 def filter_rows(raw_ref, taps_ref):
     rows = raw_ref.shape[0] * raw_ref.shape[1]
     raw = raw_ref[...].astype(jnp.float32).reshape(rows, RAW).astype(jnp.bfloat16)
-    band = jnp.broadcast_to(taps_ref[...], (TILE, SPAN))
+    taps = jnp.broadcast_to(taps_ref[...], (8, TAPS))
+    places = lax.broadcasted_iota(jnp.int32, (TAPS, SPAN), 0) + lax.broadcasted_iota(jnp.int32, (TAPS, SPAN), 1)
+    pick = jnp.where(places == TILE, 1.0, 0.0).astype(jnp.bfloat16)
+    spread = sum(contract(part, pick, 1, 0) for part in split3(taps)[::-1])
+    band = jnp.broadcast_to(spread[:1], (TILE, SPAN))
     index = lax.broadcasted_iota(jnp.int32, (TILE, SPAN), 0)
     for bit in range(7):
         band = jnp.where((index >> bit) & 1 == 1, pltpu.roll(band, DEC << bit, 1), band)
@@ -93,7 +97,12 @@
                 spectra_ref[pl.ds(start, 128, 32), :] = turned
 
 
-def stack_kernel(same, per_step, entry_ref, rows_ref, cols_ref, lag_ref, out_ref, row_spec, col_spec, cross_ref):
+def stack_kernel(same, per_step, entry_ref, rows_ref, *refs):
+    if same:
+        lag_ref, out_ref, cross_ref, row_spec = refs
+    else:
+        cols_ref, lag_ref, out_ref, cross_ref, row_spec, col_spec = refs
+
     @pl.when(pl.program_id(0) == 0)
     def _():
         arrange(rows_ref, row_spec)
@@ -123,71 +132,280 @@
         out_ref[group * 4 : group * 4 + 4] = stacked.reshape(4, TILE, LAGS).astype(jnp.bfloat16)
 
 
-def stack(gathered, entry):
+def stack(gathered, table):
     members = TILE * WINDOWS // gathered.shape[1]
     same = gathered.shape[0] == members
     per_step = 8
     block = (members,) + gathered.shape[1:]
-    spec_shape = pltpu.VMEM((2 * NBIN * WINDOWS, TILE), jnp.float32)
-    small = pltpu.VMEM((8, 128), jnp.float32)
+    spectra = pltpu.VMEM((2 * NBIN * WINDOWS, TILE), jnp.float32)
+    if same:
+        entry = table[0]
+        sides = [pl.BlockSpec(block, lambda s, entry: (0, 0, 0))]
+    else:
+        entry = table[lax.axis_index("tiles")]
+        sides = [
+            pl.BlockSpec(block, lambda s, entry: (entry[0], 0, 0)),
+            pl.BlockSpec(block, lambda s, entry: (entry[1], 0, 0)),
+        ]
     return pl.pallas_call(
         functools.partial(stack_kernel, same, per_step),
         out_shape=jax.ShapeDtypeStruct((TILE, TILE, LAGS), jnp.bfloat16),
         grid_spec=pltpu.PrefetchScalarGridSpec(
             num_scalar_prefetch=1,
             grid=(TILE // per_step,),
-            in_specs=[
-                pl.BlockSpec(block, lambda s, entry: (entry[0], 0, 0)),
-                pl.BlockSpec((8, 128) if same else block, (lambda s, entry: (0, 0)) if same else (lambda s, entry: (entry[1], 0, 0))),
-                pl.BlockSpec((2 * NBIN, LAGS), lambda s, entry: (0, 0)),
-            ],
+            in_specs=sides + [pl.BlockSpec((2 * NBIN, LAGS), lambda s, entry: (0, 0))],
             out_specs=pl.BlockSpec((per_step, TILE, LAGS), lambda s, entry: (s, 0, 0)),
-            scratch_shapes=[spec_shape, small if same else spec_shape, pltpu.VMEM((TILE * STRIDE, TILE), jnp.float32)],
+            scratch_shapes=[pltpu.VMEM((TILE * STRIDE, TILE), jnp.float32)] + [spectra] * len(sides),
         ),
         compiler_params=pltpu.CompilerParams(vmem_limit_bytes=60 << 20),
         cost_estimate=pl.CostEstimate(flops=10 << 30, bytes_accessed=12 << 20, transcendentals=0),
-    )(entry, gathered, entry_dummy() if same else gathered, lag_table())
-
-
-def entry_dummy():
-    return jnp.zeros((8, 128), jnp.float32)
-
-
-def taps_row(fir):
-    return jnp.pad(fir[::-1], (TILE + 1 - TAPS, SPAN - TILE - 1))[None, :]
-
-
-def filter_kernel(raw_ref, taps_ref, filtered_ref, sum_ref):
-    filtered = filter_rows(raw_ref, taps_ref)
-    filtered_ref[...] = filtered
-    sum_ref[...] = jnp.sum(filtered.reshape(raw_ref.shape[0], raw_ref.shape[1], SEG), 1)
-
-
-def whiten_kernel(channels, filtered_ref, sum_ref, keep_ref, table_ref, out_ref):
-    rows = filtered_ref.shape[0]
-    width = rows // WINDOWS
-    common = sum_ref[...] / channels
-    decimated = filtered_ref[...].reshape(WINDOWS, width, SEG) - common[:, None, :]
-    out_ref[...] = whiten_rows(decimated.reshape(rows, SEG), keep_ref[...], table_ref)
+    )(entry, *[gathered] * len(sides), lag_table())
+
+
+def other_core(me):
+    return me + 1 - 2 * (me % 2)
+
+
+def other_chip(me):
+    return me + 2 - 4 * ((me // 2) % 2)
+
+
+def remote(source, target, send, receive, peer):
+    return pltpu.make_async_remote_copy(
+        src_ref=source,
+        dst_ref=target,
+        send_sem=send,
+        recv_sem=receive,
+        device_id={"tiles": peer},
+        device_id_type=pl.DeviceIdType.MESH,
+    )
+
+
+def front_kernel(
+    devices, raw_ref, taps_ref, keep_ref, table_ref, out_ref,
+    sum_buf, part_buf, common_buf, held,
+    part_send, part_recv, common_send, common_recv,
+    right_send, left_send, chip_send, core_send, held_recv, local_sem,
+):
+    me = lax.axis_index("tiles")
+    channels = raw_ref.shape[1]
+    rows = WINDOWS * channels
+    barrier = pltpu.get_barrier_semaphore()
+    all_owners = devices == WINDOWS
+
+    def greet(k, carry):
+        pl.semaphore_signal(
+            barrier, inc=1, device_id={"tiles": (me + k) % devices}, device_id_type=pl.DeviceIdType.MESH
+        )
+        return carry
+
+    lax.fori_loop(1, devices, greet, 0)
+    filtered = filter_rows(raw_ref, taps_ref).reshape(WINDOWS, channels, SEG)
+    sum_buf[...] = jnp.sum(filtered, 1, keepdims=True)
+    pl.semaphore_wait(barrier, devices - 1)
+
+    def part_copy(owner, slot):
+        return remote(sum_buf.at[owner], part_buf.at[slot], part_send.at[owner], part_recv.at[slot], owner)
+
+    def common_copy(owner, peer):
+        return remote(common_buf.at[owner], common_buf.at[owner], common_send.at[peer], common_recv.at[owner], peer)
+
+    def send_part(k, carry):
+        owner = (me + k) % WINDOWS
+
+        @pl.when(owner != me)
+        def _():
+            part_copy(owner, me).start()
+
+        return carry
+
+    lax.fori_loop(1 if all_owners else 0, WINDOWS, send_part, 0)
+
+    @pl.when(me < WINDOWS)
+    def _():
+        part_buf[me] = sum_buf[me]
+
+        def take(k, carry):
+            part_copy(me, (me + k) % devices).wait_recv()
+            return carry
+
+        lax.fori_loop(1, devices, take, 0)
+        common_buf[me] = jnp.sum(part_buf[...], 0)
+
+        def give(k, carry):
+            common_copy(me, (me + k) % devices).start()
+            return carry
+
+        lax.fori_loop(1, devices, give, 0)
+
+    def take_common(k, carry):
+        owner = (me + k) % WINDOWS
+
+        @pl.when(owner != me)
+        def _():
+            common_copy(owner, me).wait_recv()
+
+        return carry
+
+    lax.fori_loop(1 if all_owners else 0, WINDOWS, take_common, 0)
+    common = common_buf[...] / (channels * devices)
+    decimated = (filtered - common).reshape(rows, SEG)
+    keep = jnp.broadcast_to(keep_ref[...].astype(jnp.float32)[:, :, None], (WINDOWS, channels, NBIN))
+    held[me] = whiten_rows(decimated, keep.reshape(rows, NBIN), table_ref)
+
+    depth = devices // 4
+    q, low = me // 4, me % 4
+    chip, core = other_chip(me), other_core(me)
+
+    def block_copy(block, send, peer):
+        return remote(held.at[block], held.at[block], send, held_recv.at[block], peer)
+
+    def to_right(level):
+        return block_copy(4 * level + low, right_send.at[level], (me + 4) % devices)
+
+    def to_left(level):
+        return block_copy(4 * level + low, left_send.at[level], (me + devices - 4) % devices)
+
+    def to_chip(level):
+        return block_copy(4 * level + low, chip_send.at[level], chip)
+
+    def to_core(block):
+        return block_copy(block, core_send.at[block // 2], core)
+
+    def arrived(block):
+        block_copy(block, core_send.at[block // 2], core).wait_recv()
+        keep_block(block)
+
+    def keep_block(block):
+        pltpu.make_async_copy(held.at[block], out_ref.at[block], local_sem.at[block]).start()
+
+    def line_block(level, forward, go):
+        block = 4 * level + low
+        arrived(block)
+
+        @pl.when(go)
+        def _():
+            forward(level).start()
+
+        to_chip(level).start()
+        to_core(block).start()
+
+    def chip_block(level):
+        block = 4 * level + other_chip(low)
+        arrived(block)
+        to_core(block).start()
+
+    @pl.when(q < depth - 1)
+    def _():
+        to_right(q).start()
+
+    @pl.when(q > 0)
+    def _():
+        to_left(q).start()
+
+    to_chip(q).start()
+    to_core(me).start()
+    keep_block(me)
+
+    def step(d, carry):
+        @pl.when(q - d >= 0)
+        def _():
+            line_block(q - d, to_right, q < depth - 1)
+
+        @pl.when(q + d < depth)
+        def _():
+            line_block(q + d, to_left, q > 0)
+
+        @pl.when(d == 1)
+        def _():
+            chip_block(q)
+
+        @pl.when((d > 1) & (q - d + 1 >= 0))
+        def _():
+            chip_block(q - d + 1)
+
+        @pl.when((d > 1) & (q + d - 1 < depth))
+        def _():
+            chip_block(q + d - 1)
+
+        return carry
+
+    lax.fori_loop(1, depth + 1, step, 0)
+
+    def from_core(pair, carry):
+        arrived(2 * pair + core % 2)
+        return carry
+
+    lax.fori_loop(0, 2 * depth, from_core, 0)
+
+    def finish(level, carry):
+        @pl.when((level <= q) & (q < depth - 1))
+        def _():
+            to_right(level).wait_send()
+
+        @pl.when((level >= q) & (q > 0))
+        def _():
+            to_left(level).wait_send()
+
+        to_chip(level).wait_send()
+        to_core(4 * level + low).wait_send()
+        to_core(4 * level + other_chip(low)).wait_send()
+        return carry
+
+    lax.fori_loop(0, depth, finish, 0)
+
+    def drain_part(k, carry):
+        owner = (me + k) % WINDOWS
+
+        @pl.when(owner != me)
+        def _():
+            part_copy(owner, me).wait_send()
+
+        return carry
+
+    lax.fori_loop(1 if all_owners else 0, WINDOWS, drain_part, 0)
+
+    @pl.when(me < WINDOWS)
+    def _():
+        def drain(k, carry):
+            common_copy(me, (me + k) % devices).wait_send()
+            return carry
+
+        lax.fori_loop(1, devices, drain, 0)
+
+    def settle(block, carry):
+        pltpu.make_async_copy(held.at[block], out_ref.at[block], local_sem.at[block]).wait()
+        return carry
+
+    lax.fori_loop(0, devices, settle, 0)
+
+
+def front(devices, raw, fir, keep):
+    rows = raw.shape[0] * raw.shape[1]
+    depth = devices // 4
+    dma = pltpu.SemaphoreType.DMA
+    vmem = pl.BlockSpec(memory_space=pltpu.VMEM)
+    line = pltpu.VMEM((WINDOWS, 1, SEG), jnp.float32)
+    return pl.pallas_call(
+        functools.partial(front_kernel, devices),
+        out_shape=jax.ShapeDtypeStruct((devices, rows, 2 * NBIN), jnp.bfloat16),
+        in_specs=[vmem] * 4,
+        out_specs=pl.BlockSpec(memory_space=pl.ANY),
+        scratch_shapes=[
+            line, pltpu.VMEM((devices, 1, SEG), jnp.float32), line,
+            pltpu.VMEM((devices, rows, 2 * NBIN), jnp.bfloat16),
+            dma((WINDOWS,)), dma((devices,)), dma((devices,)), dma((WINDOWS,)),
+            dma((depth,)), dma((depth,)), dma((depth,)), dma((2 * depth,)), dma((devices,)), dma((devices,)),
+        ],
+        compiler_params=pltpu.CompilerParams(
+            collective_id=0, has_side_effects=True, vmem_limit_bytes=48 << 20
+        ),
+    )(raw, fir.reshape(1, TAPS), keep, dft_tables())
 
 
 def local(raw, fir, keep, table):
-    devices = lax.axis_size("tiles")
-    rows = raw.shape[0] * raw.shape[1]
-    filtered, sums = pl.pallas_call(
-        filter_kernel,
-        out_shape=(jax.ShapeDtypeStruct((rows, SEG), jnp.float32), jax.ShapeDtypeStruct((WINDOWS, SEG), jnp.float32)),
-        compiler_params=pltpu.CompilerParams(vmem_limit_bytes=32 << 20),
-    )(raw, taps_row(fir))
-    sums = lax.psum(sums, "tiles")
-    whitened = pl.pallas_call(
-        functools.partial(whiten_kernel, raw.shape[1] * devices),
-        out_shape=jax.ShapeDtypeStruct((rows, 2 * NBIN), jnp.bfloat16),
-        compiler_params=pltpu.CompilerParams(vmem_limit_bytes=32 << 20),
-    )(filtered, sums, keep.reshape(rows, 1), dft_tables())
-    gathered = lax.all_gather(whitened, "tiles", axis=0)
-    entry = table[lax.axis_index("tiles")]
-    return stack(gathered, entry)[None]
+    gathered = front(lax.axis_size("tiles"), raw, fir, keep)
+    return stack(gathered, table)[None]
 
 
 def solution(mesh):

time: 150 us -> 69 us (0.46)
  blocking collectives: 62.9 us -> 0 us
  waiting for transfers between devices: 38.2 us -> 0 us
  Pallas kernels: 29.8 us -> 62.3 us
  between operations: 13.4 us -> 0.02 us
    psum x1 -> x0, blocking collectives: 62.9 us -> none  [local(): sums = lax.psum(sums, 'tiles')]
    all_gather x1 -> x0, waiting for transfers between devices: 38.2 us -> none  [local(): gathered = lax.all_gather(whitened, 'tiles', axis=0)]
    pallas_call x2 -> x1, Pallas kernels: 2.28 us -> 34.8 us  [front(): pl.pallas_call(functools.partial(front_kernel, devices), out_shape=jax.Sh...]
    unnamed x7 -> x9, local copies, waits for them, and re-layouts: 3.02 us -> 5.01 us
  transfers between devices with their start and end apart: 1 -> 0, of which waited for: 1 -> 0; matrix products, arithmetic and copies ran while one was open for 0% -> 0% of each run, Pallas kernels for 0% -> 0%
where the time goes in v2:
time: 69 us; the launch traced here: 68.7 us
  Pallas kernels  62.3 us (90%)
  local copies, waits for them, and re-layouts  6.32 us (9%)
    pallas_call x1, Pallas kernels, front(): pl.pallas_call(functools.partial(front_kernel, devices), out_shape=jax.Sh...  34.8 us
    pallas_call x1, Pallas kernels, stack(): pl.pallas_call(functools.partial(stack_kernel, same, per_step), out_shape...  27.5 us
    unnamed x9, local copies, waits for them, and re-layouts  5.01 us

profile of v2, /device:TPU:0, one launch (start us, length us, event | category | flops | bytes accessed | tf_op | source)
XLA Modules:
  0.0 68.7 jit_solution(13804218575030621557)
XLA Ops:
  0.0 1.3 %slice_reduce_fusion.entry_ref = s32[2]{0:T(128)} fusion(s32[16,2]{0,1:T(2,128)} %param.9), kind=kLoop, calls=%fused_computation | loop fusion | bytes 16 | tf_op jit(solution)/shard_map/slice | solution.py:142
  1.3 0.8 %copy.7.keep_ref = s32[16,8]{1,0:T(8,128)S(1)} copy(s32[16,8]{0,1:T(8,128)} %param.8) | data formatting | bytes 1024 | tf_op args[2]
  2.1 0.0 copy-start.1
  2.1 1.2 %copy-done.1 = bf16[1024,512]{1,0:T(8,128)(2,1)S(1)} copy-done((bf16[1024,512]{1,0:T(8,128)(2,1)S(1)}, bf16[1024,512]{1,0:T(8,128)(2,1)}, u32[]{:S(2)}) %copy-start.1) | copy-done | bytes 1048600
  3.3 0.0 copy-start.2
  3.3 1.0 %copy-done.2 = bf16[16,8,2048]{2,1,0:T(8,128)(2,1)S(1)} copy-done((bf16[16,8,2048]{2,1,0:T(8,128)(2,1)S(1)}, bf16[16,8,2048]{2,1,0:T(8,128)(2,1)}, u32[]{:S(2)}) %copy-start.2) | copy-done | bytes 524312
  4.3 0.0 copy-start.3
  4.3 0.7 copy-done.3
  5.0 34.8 %shard_map.64.rows_ref = bf16[16,128,512]{2,1,0:T(8,128)(2,1)S(1)} custom-call(bf16[16,8,2048]{2,1,0:T(8,128)(2,1)S(1)} %copy-done.2, f32[1,64]{1,0:T(1,128)S(1)} %bitcast.2, s32[16,8]{1,0:T(8,128)S(1)} %copy.7.keep_ref, bf16[1024,512]{1,0:T(8,128)(2,1)S(1)} %copy-done.1), custom_call_target="tpu_custom_call" | custom-call | tf_op jit(solution)/shard_map/pallas_call | solution.py:389
  39.8 0.0 copy-start
  39.8 1.3 %copy-done = bf16[16,128,512]{2,1,0:T(8,128)(2,1)} copy-done((bf16[16,128,512]{2,1,0:T(8,128)(2,1)}, bf16[16,128,512]{2,1,0:T(8,128)(2,1)S(1)}, u32[]{:S(2)}) %copy-start) | copy-done | bytes 2097176
  41.2 27.5 %shard_map.65 = bf16[128,128,256]{2,1,0:T(8,128)(2,1)} custom-call(s32[2]{0:T(128)} %slice_reduce_fusion.entry_ref, bf16[16,128,512]{2,1,0:T(8,128)(2,1)} %copy-done, bf16[512,256]{1,0:T(8,128)(2,1)} %constant.5.clone.refs_0_), custom_call_target="tpu_custom_call" | custom-call | flops 10737418240 | bytes 12582912 | tf_op jit(solution)/shard_map/pallas_call | solution.py:150
Async XLA Ops:
  2.1 1.2 %copy-start.1 = (bf16[1024,512]{1,0:T(8,128)(2,1)S(1)}, bf16[1024,512]{1,0:T(8,128)(2,1)}, u32[]{:S(2)}) copy-start(bf16[1024,512]{1,0:T(8,128)(2,1)} %constant.4.clone.table_ref) | copy-start | bytes 3145732
  3.3 1.0 %copy-start.2 = (bf16[16,8,2048]{2,1,0:T(8,128)(2,1)S(1)}, bf16[16,8,2048]{2,1,0:T(8,128)(2,1)}, u32[]{:S(2)}) copy-start(bf16[16,8,2048]{2,1,0:T(8,128)(2,1)} %raw_ref.1) | copy-start | bytes 1572868
  4.3 0.7 copy-start.3
  39.8 1.3 %copy-start = (bf16[16,128,512]{2,1,0:T(8,128)(2,1)}, bf16[16,128,512]{2,1,0:T(8,128)(2,1)S(1)}, u32[]{:S(2)}) copy-start(bf16[16,128,512]{2,1,0:T(8,128)(2,1)S(1)} %shard_map.64.rows_ref) | copy-start | bytes 6291460

commit v3 on v2

--- a/solution.py
+++ b/solution.py
@@ -18,6 +18,7 @@
 NBIN = 256
 SPAN = 640
 STRIDE = 520
+PIECES = 2
 
 
 def split2(x):
@@ -120,7 +121,7 @@
             cross_ref[pl.ds(f + NBIN, TILE, STRIDE), :] = cross[:, TILE:]
             return carry
 
-        lax.fori_loop(0, NBIN, one_bin, 0, unroll=8)
+        lax.fori_loop(0, NBIN, one_bin, 0, unroll=64)
 
     base = pl.program_id(0) * per_step
     for group in range(per_step // 4):
@@ -135,11 +136,11 @@
 def stack(gathered, table):
     members = TILE * WINDOWS // gathered.shape[1]
     same = gathered.shape[0] == members
-    per_step = 8
+    per_step = 32
     block = (members,) + gathered.shape[1:]
     spectra = pltpu.VMEM((2 * NBIN * WINDOWS, TILE), jnp.float32)
     if same:
-        entry = table[0]
+        entry = table
         sides = [pl.BlockSpec(block, lambda s, entry: (0, 0, 0))]
     else:
         entry = table[lax.axis_index("tiles")]
@@ -182,8 +183,8 @@
 
 
 def front_kernel(
-    devices, raw_ref, taps_ref, keep_ref, table_ref, out_ref,
-    sum_buf, part_buf, common_buf, held,
+    devices, raw_hbm, taps_ref, keep_ref, table_hbm, out_ref,
+    raw_ref, table_ref, load_sem, sum_buf, part_buf, common_buf, held,
     part_send, part_recv, common_send, common_recv,
     right_send, left_send, chip_send, core_send, held_recv, local_sem,
 ):
@@ -199,7 +200,12 @@
         )
         return carry
 
+    load_raw = pltpu.make_async_copy(raw_hbm, raw_ref, load_sem.at[0])
+    load_raw.start()
+    load_table = pltpu.make_async_copy(table_hbm, table_ref, load_sem.at[1])
+    load_table.start()
     lax.fori_loop(1, devices, greet, 0)
+    load_raw.wait()
     filtered = filter_rows(raw_ref, taps_ref).reshape(WINDOWS, channels, SEG)
     sum_buf[...] = jnp.sum(filtered, 1, keepdims=True)
     pl.semaphore_wait(barrier, devices - 1)
@@ -251,105 +257,117 @@
     common = common_buf[...] / (channels * devices)
     decimated = (filtered - common).reshape(rows, SEG)
     keep = jnp.broadcast_to(keep_ref[...].astype(jnp.float32)[:, :, None], (WINDOWS, channels, NBIN))
-    held[me] = whiten_rows(decimated, keep.reshape(rows, NBIN), table_ref)
+    load_table.wait()
+    whitened = whiten_rows(decimated, keep.reshape(rows, NBIN), table_ref)
+    held[me] = whitened.reshape(PIECES, rows // PIECES, 2 * NBIN)
 
     depth = devices // 4
     q, low = me // 4, me % 4
     chip, core = other_chip(me), other_core(me)
 
-    def block_copy(block, send, peer):
-        return remote(held.at[block], held.at[block], send, held_recv.at[block], peer)
-
-    def to_right(level):
-        return block_copy(4 * level + low, right_send.at[level], (me + 4) % devices)
-
-    def to_left(level):
-        return block_copy(4 * level + low, left_send.at[level], (me + devices - 4) % devices)
-
-    def to_chip(level):
-        return block_copy(4 * level + low, chip_send.at[level], chip)
-
-    def to_core(block):
-        return block_copy(block, core_send.at[block // 2], core)
-
-    def arrived(block):
-        block_copy(block, core_send.at[block // 2], core).wait_recv()
-        keep_block(block)
-
-    def keep_block(block):
-        pltpu.make_async_copy(held.at[block], out_ref.at[block], local_sem.at[block]).start()
-
-    def line_block(level, forward, go):
+    def block_copy(block, piece, send, peer):
+        return remote(held.at[block, piece], held.at[block, piece], send, held_recv.at[block, piece], peer)
+
+    def to_right(level, piece):
+        return block_copy(4 * level + low, piece, right_send.at[level, piece], (me + 4) % devices)
+
+    def to_left(level, piece):
+        return block_copy(4 * level + low, piece, left_send.at[level, piece], (me + devices - 4) % devices)
+
+    def to_chip(level, piece):
+        return block_copy(4 * level + low, piece, chip_send.at[level, piece], chip)
+
+    def to_core(block, piece):
+        return block_copy(block, piece, core_send.at[block // 2, piece], core)
+
+    def local_copy(block, piece):
+        part = rows // PIECES
+        return pltpu.make_async_copy(
+            held.at[block, piece], out_ref.at[block, pl.ds(piece * part, part)], local_sem.at[block, piece]
+        )
+
+    def arrived(block, piece):
+        to_core(block, piece).wait_recv()
+        local_copy(block, piece).start()
+
+    def line_block(level, piece, forward, go):
         block = 4 * level + low
-        arrived(block)
+        arrived(block, piece)
 
         @pl.when(go)
         def _():
-            forward(level).start()
-
-        to_chip(level).start()
-        to_core(block).start()
-
-    def chip_block(level):
+            forward(level, piece).start()
+
+        to_chip(level, piece).start()
+        to_core(block, piece).start()
+
+    def chip_block(level, piece):
         block = 4 * level + other_chip(low)
-        arrived(block)
-        to_core(block).start()
-
-    @pl.when(q < depth - 1)
-    def _():
-        to_right(q).start()
-
-    @pl.when(q > 0)
-    def _():
-        to_left(q).start()
-
-    to_chip(q).start()
-    to_core(me).start()
-    keep_block(me)
+        arrived(block, piece)
+        to_core(block, piece).start()
+
+    for piece in range(PIECES):
+        @pl.when(q < depth - 1)
+        def _():
+            to_right(q, piece).start()
+
+        @pl.when(q > 0)
+        def _():
+            to_left(q, piece).start()
+
+        to_chip(q, piece).start()
+
+    for piece in range(PIECES):
+        to_core(me, piece).start()
+        local_copy(me, piece).start()
 
     def step(d, carry):
-        @pl.when(q - d >= 0)
-        def _():
-            line_block(q - d, to_right, q < depth - 1)
-
-        @pl.when(q + d < depth)
-        def _():
-            line_block(q + d, to_left, q > 0)
-
-        @pl.when(d == 1)
-        def _():
-            chip_block(q)
-
-        @pl.when((d > 1) & (q - d + 1 >= 0))
-        def _():
-            chip_block(q - d + 1)
-
-        @pl.when((d > 1) & (q + d - 1 < depth))
-        def _():
-            chip_block(q + d - 1)
+        for piece in range(PIECES):
+            @pl.when(q - d >= 0)
+            def _():
+                line_block(q - d, piece, to_right, q < depth - 1)
+
+            @pl.when(q + d < depth)
+            def _():
+                line_block(q + d, piece, to_left, q > 0)
+
+        for piece in range(PIECES):
+            @pl.when(d == 1)
+            def _():
+                chip_block(q, piece)
+
+            @pl.when((d > 1) & (q - d + 1 >= 0))
+            def _():
+                chip_block(q - d + 1, piece)
+
+            @pl.when((d > 1) & (q + d - 1 < depth))
+            def _():
+                chip_block(q + d - 1, piece)
 
         return carry
 
     lax.fori_loop(1, depth + 1, step, 0)
 
     def from_core(pair, carry):
-        arrived(2 * pair + core % 2)
+        for piece in range(PIECES):
+            arrived(2 * pair + core % 2, piece)
         return carry
 
     lax.fori_loop(0, 2 * depth, from_core, 0)
 
     def finish(level, carry):
-        @pl.when((level <= q) & (q < depth - 1))
-        def _():
-            to_right(level).wait_send()
-
-        @pl.when((level >= q) & (q > 0))
-        def _():
-            to_left(level).wait_send()
-
-        to_chip(level).wait_send()
-        to_core(4 * level + low).wait_send()
-        to_core(4 * level + other_chip(low)).wait_send()
+        for piece in range(PIECES):
+            @pl.when((level <= q) & (q < depth - 1))
+            def _():
+                to_right(level, piece).wait_send()
+
+            @pl.when((level >= q) & (q > 0))
+            def _():
+                to_left(level, piece).wait_send()
+
+            to_chip(level, piece).wait_send()
+            to_core(4 * level + low, piece).wait_send()
+            to_core(4 * level + other_chip(low), piece).wait_send()
         return carry
 
     lax.fori_loop(0, depth, finish, 0)
@@ -374,7 +392,8 @@
         lax.fori_loop(1, devices, drain, 0)
 
     def settle(block, carry):
-        pltpu.make_async_copy(held.at[block], out_ref.at[block], local_sem.at[block]).wait()
+        for piece in range(PIECES):
+            local_copy(block, piece).wait()
         return carry
 
     lax.fori_loop(0, devices, settle, 0)
@@ -385,20 +404,23 @@
     depth = devices // 4
     dma = pltpu.SemaphoreType.DMA
     vmem = pl.BlockSpec(memory_space=pltpu.VMEM)
+    hbm = pl.BlockSpec(memory_space=pl.ANY)
     line = pltpu.VMEM((WINDOWS, 1, SEG), jnp.float32)
     return pl.pallas_call(
         functools.partial(front_kernel, devices),
         out_shape=jax.ShapeDtypeStruct((devices, rows, 2 * NBIN), jnp.bfloat16),
-        in_specs=[vmem] * 4,
+        in_specs=[hbm, vmem, vmem, hbm],
         out_specs=pl.BlockSpec(memory_space=pl.ANY),
         scratch_shapes=[
+            pltpu.VMEM(raw.shape, jnp.bfloat16), pltpu.VMEM((2 * SEG, 2 * NBIN), jnp.bfloat16), dma((2,)),
             line, pltpu.VMEM((devices, 1, SEG), jnp.float32), line,
-            pltpu.VMEM((devices, rows, 2 * NBIN), jnp.bfloat16),
+            pltpu.VMEM((devices, PIECES, rows // PIECES, 2 * NBIN), jnp.bfloat16),
             dma((WINDOWS,)), dma((devices,)), dma((devices,)), dma((WINDOWS,)),
-            dma((depth,)), dma((depth,)), dma((depth,)), dma((2 * depth,)), dma((devices,)), dma((devices,)),
+            dma((depth, PIECES)), dma((depth, PIECES)), dma((depth, PIECES)), dma((2 * depth, PIECES)),
+            dma((devices, PIECES)), dma((devices, PIECES)),
         ],
         compiler_params=pltpu.CompilerParams(
-            collective_id=0, has_side_effects=True, vmem_limit_bytes=48 << 20
+            collective_id=0, has_side_effects=True, vmem_limit_bytes=60 << 20
         ),
     )(raw, fir.reshape(1, TAPS), keep, dft_tables())
 

time: 69 us -> 54.9 us (0.80)
  Pallas kernels: 62.3 us -> 51.8 us
  local copies, waits for them, and re-layouts: 6.32 us -> 2.7 us
    pallas_call x1, Pallas kernels: 27.5 us -> 18.2 us  [stack(): pl.pallas_call(functools.partial(stack_kernel, same, per_step), out_shape...]
    unnamed x9 -> x2, local copies, waits for them, and re-layouts: 5.01 us -> 2.7 us
    slice x1 -> x0, local copies, waits for them, and re-layouts: 1.31 us -> none  [stack(): entry = table[0]]
    pallas_call x1, Pallas kernels: 34.8 us -> 33.6 us  [front(): pl.pallas_call(functools.partial(front_kernel, devices), out_shape=jax.Sh...]
where the time goes in v3:
time: 54.9 us; the launch traced here: 54.5 us
  Pallas kernels  51.8 us (94%)
  local copies, waits for them, and re-layouts  2.7 us (5%)
    pallas_call x1, Pallas kernels, front(): pl.pallas_call(functools.partial(front_kernel, devices), out_shape=jax.Sh...  33.6 us
    pallas_call x1, Pallas kernels, stack(): pl.pallas_call(functools.partial(stack_kernel, same, per_step), out_shape...  18.2 us
    unnamed x2, local copies, waits for them, and re-layouts  2.7 us

profile of v3, /device:TPU:0, one launch (start us, length us, event | category | flops | bytes accessed | tf_op | source)
XLA Modules:
  0.0 54.5 jit_solution(13227368764457227821)
XLA Ops:
  0.0 1.4 %copy.7.keep_ref = s32[16,8]{1,0:T(8,128)} copy(s32[16,8]{0,1:T(8,128)} %param.8) | data formatting | bytes 1024 | tf_op args[2]
  1.4 1.3 %copy.8.entry_ref = s32[16,2]{1,0:T(8,128)} copy(s32[16,2]{0,1:T(2,128)} %param.9) | data formatting | bytes 256 | tf_op args[3]
  2.7 33.6 %shard_map.64.rows_ref = bf16[16,128,512]{2,1,0:T(8,128)(2,1)} custom-call(bf16[16,8,2048]{2,1,0:T(8,128)(2,1)} %raw_hbm.1, f32[1,64]{1,0:T(1,128)} %bitcast.2, s32[16,8]{1,0:T(8,128)} %copy.7.keep_ref, bf16[1024,512]{1,0:T(8,128)(2,1)} %constant.4.clone.table_hbm), custom_call_target="tpu_custom_call" | custom-call | tf_op jit(solution)/shard_map/pallas_call | solution.py:409
  36.3 18.2 %shard_map.65 = bf16[128,128,256]{2,1,0:T(8,128)(2,1)} custom-call(s32[16,2]{1,0:T(8,128)} %copy.8.entry_ref, bf16[16,128,512]{2,1,0:T(8,128)(2,1)} %shard_map.64.rows_ref, bf16[512,256]{1,0:T(8,128)(2,1)} %constant.5.clone.refs_0_), custom_call_target="tpu_custom_call" | custom-call | flops 10737418240 | bytes 12582912 | tf_op jit(solution)/shard_map/pallas_call | solution.py:151

commit v4 on v3

--- a/solution.py
+++ b/solution.py
@@ -98,11 +98,11 @@
                 spectra_ref[pl.ds(start, 128, 32), :] = turned
 
 
-def stack_kernel(same, per_step, entry_ref, rows_ref, *refs):
+def stack_kernel(same, per_step, *refs):
     if same:
-        lag_ref, out_ref, cross_ref, row_spec = refs
+        rows_ref, lag_ref, out_ref, cross_ref, row_spec = refs
     else:
-        cols_ref, lag_ref, out_ref, cross_ref, row_spec, col_spec = refs
+        _, rows_ref, cols_ref, lag_ref, out_ref, cross_ref, row_spec, col_spec = refs
 
     @pl.when(pl.program_id(0) == 0)
     def _():
@@ -140,10 +140,10 @@
     block = (members,) + gathered.shape[1:]
     spectra = pltpu.VMEM((2 * NBIN * WINDOWS, TILE), jnp.float32)
     if same:
-        entry = table
-        sides = [pl.BlockSpec(block, lambda s, entry: (0, 0, 0))]
+        prefetch = []
+        sides = [pl.BlockSpec(block, lambda s: (0, 0, 0))]
     else:
-        entry = table[lax.axis_index("tiles")]
+        prefetch = [table[lax.axis_index("tiles")]]
         sides = [
             pl.BlockSpec(block, lambda s, entry: (entry[0], 0, 0)),
             pl.BlockSpec(block, lambda s, entry: (entry[1], 0, 0)),
@@ -152,15 +152,15 @@
         functools.partial(stack_kernel, same, per_step),
         out_shape=jax.ShapeDtypeStruct((TILE, TILE, LAGS), jnp.bfloat16),
         grid_spec=pltpu.PrefetchScalarGridSpec(
-            num_scalar_prefetch=1,
+            num_scalar_prefetch=len(prefetch),
             grid=(TILE // per_step,),
-            in_specs=sides + [pl.BlockSpec((2 * NBIN, LAGS), lambda s, entry: (0, 0))],
-            out_specs=pl.BlockSpec((per_step, TILE, LAGS), lambda s, entry: (s, 0, 0)),
+            in_specs=sides + [pl.BlockSpec((2 * NBIN, LAGS), lambda s, *entry: (0, 0))],
+            out_specs=pl.BlockSpec((per_step, TILE, LAGS), lambda s, *entry: (s, 0, 0)),
             scratch_shapes=[pltpu.VMEM((TILE * STRIDE, TILE), jnp.float32)] + [spectra] * len(sides),
         ),
         compiler_params=pltpu.CompilerParams(vmem_limit_bytes=60 << 20),
         cost_estimate=pl.CostEstimate(flops=10 << 30, bytes_accessed=12 << 20, transcendentals=0),
-    )(entry, *[gathered] * len(sides), lag_table())
+    )(*prefetch, *[gathered] * len(sides), lag_table())
 
 
 def other_core(me):
@@ -256,7 +256,7 @@
     lax.fori_loop(1 if all_owners else 0, WINDOWS, take_common, 0)
     common = common_buf[...] / (channels * devices)
     decimated = (filtered - common).reshape(rows, SEG)
-    keep = jnp.broadcast_to(keep_ref[...].astype(jnp.float32)[:, :, None], (WINDOWS, channels, NBIN))
+    keep = jnp.broadcast_to(keep_ref[...].astype(jnp.float32).T[:, :, None], (WINDOWS, channels, NBIN))
     load_table.wait()
     whitened = whiten_rows(decimated, keep.reshape(rows, NBIN), table_ref)
     held[me] = whitened.reshape(PIECES, rows // PIECES, 2 * NBIN)
@@ -422,7 +422,7 @@
         compiler_params=pltpu.CompilerParams(
             collective_id=0, has_side_effects=True, vmem_limit_bytes=60 << 20
         ),
-    )(raw, fir.reshape(1, TAPS), keep, dft_tables())
+    )(raw, fir.reshape(1, TAPS), keep.T, dft_tables())
 
 
 def local(raw, fir, keep, table):

time: 54.9 us -> 51.4 us (0.936)
  local copies, waits for them, and re-layouts: 2.7 us -> 0 us
  Pallas kernels: 51.8 us -> 51.1 us
    unnamed x2 -> x0, local copies, waits for them, and re-layouts: 2.7 us -> none
    pallas_call x1, Pallas kernels: 18.2 us -> 17.4 us  [stack(): pl.pallas_call(functools.partial(stack_kernel, same, per_step), out_shape...]
where the time goes in v4:
time: 51.4 us; the launch traced here: 51.1 us
  Pallas kernels  51.1 us (99%)
    pallas_call x1, Pallas kernels, front(): pl.pallas_call(functools.partial(front_kernel, devices), out_shape=jax.Sh...  33.7 us
    pallas_call x1, Pallas kernels, stack(): pl.pallas_call(functools.partial(stack_kernel, same, per_step), out_shape...  17.4 us

profile of v4, /device:TPU:0, one launch (start us, length us, event | category | flops | bytes accessed | tf_op | source)
XLA Modules:
  0.0 51.1 jit_solution(11198712681626132907)
XLA Ops:
  0.0 33.7 %shard_map.55.refs_0_ = bf16[16,128,512]{2,1,0:T(8,128)(2,1)} custom-call(bf16[16,8,2048]{2,1,0:T(8,128)(2,1)} %raw_hbm.1, f32[1,64]{1,0:T(1,128)} %bitcast.4, s32[8,16]{1,0:T(8,128)} %bitcast.3, bf16[1024,512]{1,0:T(8,128)(2,1)} %constant.4.clone.table_hbm), custom_call_target="tpu_custom_call" | custom-call | tf_op jit(solution)/shard_map/pallas_call | solution.py:409
  33.7 17.4 %shard_map.56 = bf16[128,128,256]{2,1,0:T(8,128)(2,1)} custom-call(bf16[16,128,512]{2,1,0:T(8,128)(2,1)} %shard_map.55.refs_0_, bf16[512,256]{1,0:T(8,128)(2,1)} %constant.5.clone.refs_1_), custom_call_target="tpu_custom_call" | custom-call | flops 10737418240 | bytes 12582912 | tf_op jit(solution)/shard_map/pallas_call | solution.py:151

commit v5 on v4

--- a/solution.py
+++ b/solution.py
@@ -18,7 +18,7 @@
 NBIN = 256
 SPAN = 640
 STRIDE = 520
-PIECES = 2
+PIECES = 4
 
 
 def split2(x):
@@ -200,11 +200,11 @@
         )
         return carry
 
+    lax.fori_loop(1, devices, greet, 0)
     load_raw = pltpu.make_async_copy(raw_hbm, raw_ref, load_sem.at[0])
     load_raw.start()
     load_table = pltpu.make_async_copy(table_hbm, table_ref, load_sem.at[1])
     load_table.start()
-    lax.fori_loop(1, devices, greet, 0)
     load_raw.wait()
     filtered = filter_rows(raw_ref, taps_ref).reshape(WINDOWS, channels, SEG)
     sum_buf[...] = jnp.sum(filtered, 1, keepdims=True)

time: 51.4 us -> 51 us (level)
  no operation moved by 1% of the time
where the time goes in v5:
time: 51 us; the launch traced here: 50.6 us
  Pallas kernels  50.6 us (99%)
    pallas_call x1, Pallas kernels, front(): pl.pallas_call(functools.partial(front_kernel, devices), out_shape=jax.Sh...  33.2 us
    pallas_call x1, Pallas kernels, stack(): pl.pallas_call(functools.partial(stack_kernel, same, per_step), out_shape...  17.4 us

profile of v5, /device:TPU:0, one launch (start us, length us, event | category | flops | bytes accessed | tf_op | source)
XLA Modules:
  0.0 50.6 jit_solution(2641152044710117192)
XLA Ops:
  0.0 33.2 %shard_map.55.refs_0_ = bf16[16,128,512]{2,1,0:T(8,128)(2,1)} custom-call(bf16[16,8,2048]{2,1,0:T(8,128)(2,1)} %raw_hbm.1, f32[1,64]{1,0:T(1,128)} %bitcast.4, s32[8,16]{1,0:T(8,128)} %bitcast.3, bf16[1024,512]{1,0:T(8,128)(2,1)} %constant.4.clone.table_hbm), custom_call_target="tpu_custom_call" | custom-call | tf_op jit(solution)/shard_map/pallas_call | solution.py:409
  33.2 17.4 %shard_map.56 = bf16[128,128,256]{2,1,0:T(8,128)(2,1)} custom-call(bf16[16,128,512]{2,1,0:T(8,128)(2,1)} %shard_map.55.refs_0_, bf16[512,256]{1,0:T(8,128)(2,1)} %constant.5.clone.refs_1_), custom_call_target="tpu_custom_call" | custom-call | flops 10737418240 | bytes 12582912 | tf_op jit(solution)/shard_map/pallas_call | solution.py:151
